TPU v7x, 128 devices: a whole 4x4x4 slice. The times are simulated.
128 devices in a mesh: row: 16 (over x, y), col: 8 (over z, core).
Axes of the slice: x: 4, y: 4, z: 4, core: 2. Of those that a mesh axis runs over, the one named last changes fastest.
Arguments:
- features: float32 [32768, 256], P(('row', 'col')), may hold values from -6 to 6
- new_features: float32 [8192, 256], P(('row', 'col')), may hold values from -6 to 6
- lengths: int32 [32768], P(('row', 'col')), may hold values from 1 to 64
- targets: float32 [32768, 64], P(('row', 'col')), may hold values from -6 to 6
- prior_train: float32 [32768, 256], P(('row', 'col')), may hold values from -6 to 6
- noise_draw: float32 [32768, 256], P(('row', 'col')), may hold values from -6 to 6
- prior_new: float32 [8192, 256], P(('row', 'col')), may hold values from -6 to 6
- time_kernel: float32 [64, 64], replicated, may hold values from -16 to 16.5, as said below
- noise_var: float32 [64], replicated, may hold values from 0.05 to 0.5
Outputs:
- residual: float32 [32768, 256], P(('row', 'col'))
- predicted: float32 [8192, 256], P(('row', 'col'))
Inputs may be any that keep to these rules, and one draw needn't show every extreme that they name: `time_kernel`: symmetric positive definite.
All inputs are finite; a program needn't handle non-finite values.
Results may differ from a plain program's by a relative error of at most 0.00022.
Values sent between devices are 32-bit elements; how exact they have to be, the bound alone decides.
No kernel may reach another device: no remote copies, remote signals or barrier semaphores. Data moves between devices by JAX's collectives and lax.ppermute only.
A program may use at most 128 MiB of HBM per device.

v0:
```python
import jax
import jax.numpy as jnp
from jax import lax
from jax.sharding import PartitionSpec as P

ITERS = 2


def unit_rows(values):
    return values / jnp.sqrt(jnp.sum(values * values, axis=1, keepdims=True) + 1e-06)


def kernel(left, right):
    inner = lax.dot_general(left, right, (((1,), (1,)), ((), ())), precision=lax.Precision.HIGHEST)
    return inner + inner * inner * inner


def shards(
    features,
    new_features,
    lengths,
    targets,
    prior_train,
    noise_draw,
    prior_new,
    time_kernel,
    noise_var,
):
    checkpoints = time_kernel.shape[0]
    samples = prior_train.shape[1] // checkpoints
    normed = unit_rows(features)
    normed_new = unit_rows(new_features)
    row_block, row_new = (
        lax.all_gather(normed, "col", axis=0, tiled=True),
        lax.all_gather(normed_new, "col", axis=0, tiled=True),
    )
    column_set = lax.all_gather(normed, "row", axis=0, tiled=True)
    mixing = jnp.kron(jnp.eye(samples, dtype=jnp.float32), time_kernel)
    position = jnp.arange(samples * checkpoints, dtype=jnp.int32) % checkpoints
    mask = (position[None, :] < lengths[:, None]).astype(jnp.float32)
    noise_cols = jnp.tile(noise_var, samples)
    rhs = mask * (jnp.tile(targets, (1, samples)) - prior_train - jnp.sqrt(noise_cols) * noise_draw)
    kernel_tile = kernel(row_block, column_set)

    def per_sample(first, second):
        return jnp.sum((first * second).reshape(first.shape[0], samples, checkpoints), axis=(0, 2))

    def squares(values):
        return lax.psum(per_sample(values, values), ("row", "col"))

    solution = jnp.zeros_like(rhs)
    residual = rhs
    direction = rhs
    norm_now = squares(residual)
    for step in range(ITERS):
        mixed = jnp.dot(direction, mixing, precision=lax.Precision.HIGHEST)
        spread = lax.all_gather(mixed, "row", axis=0, tiled=True)
        product = lax.psum_scatter(
            jnp.dot(kernel_tile, spread, precision=lax.Precision.HIGHEST),
            "col",
            scatter_dimension=0,
            tiled=True,
        )
        image = mask * product + noise_cols * direction
        curve = lax.psum(per_sample(direction, image), ("row", "col"))
        alpha = jnp.repeat(norm_now / curve, checkpoints)
        solution = solution + alpha * direction
        residual = residual - alpha * image
        if step + 1 < ITERS:
            norm_next = squares(residual)
            direction = residual + jnp.repeat(norm_next / norm_now, checkpoints) * direction
            norm_now = norm_next
    mixed_solution = jnp.dot(solution, mixing, precision=lax.Precision.HIGHEST)
    gathered = lax.all_gather(mixed_solution, "row", axis=0, tiled=True)
    cross = kernel(row_new, column_set)
    predicted = prior_new + lax.psum_scatter(
        jnp.dot(cross, gathered, precision=lax.Precision.HIGHEST),
        "col",
        scatter_dimension=0,
        tiled=True,
    )
    return (residual, predicted)


def solution(mesh):
    return jax.shard_map(
        shards,
        mesh=mesh,
        in_specs=(
            P(("row", "col"), None),
            P(("row", "col"), None),
            P(("row", "col")),
            P(("row", "col"), None),
            P(("row", "col"), None),
            P(("row", "col"), None),
            P(("row", "col"), None),
            P(),
            P(),
        ),
        out_specs=(P(("row", "col"), None), P(("row", "col"), None)),
        check_vma=False,
    )
```

profile of v0, /device:TPU:0, one launch (start us, length us, event | category | flops | bytes accessed | tf_op | source)
XLA Modules:
  0.0 626.6 jit_solution(7220657233495623977)
XLA Ops:
  8.3 1.8 broadcast_divide_fusion
  13.9 1.1 compare_select_fusion.2
  16.2 22.0 %all-gather.6.cloned.1.call-done = f32[2048,256]{1,0:T(8,128)} async-done(((f32[256,256]{1,0:T(8,128)}), f32[2048,256]{1,0:T(8,128)}) %all-gather.6.cloned.1.call-update) | async-done | bytes 2097168 | tf_op jit(solution)/shard_map/all_gather | solution.py:34
  38.2 53.7 %all-gather.8.cloned.1.call-done = f32[4096,256]{1,0:T(8,128)} async-done(((f32[256,256]{1,0:T(8,128)}), f32[4096,256]{1,0:T(8,128)}) %all-gather.8.cloned.1.call-update) | async-done | bytes 4194320 | tf_op jit(solution)/shard_map/all_gather | solution.py:37
  91.9 32.7 %fusion.13 = f32[2048,4096]{1,0:T(8,128)} fusion(f32[2048,256]{1,0:T(8,128)} %all-gather.6.cloned.1.call-done, f32[4096,256]{1,0:T(8,128)} %all-gather.8.cloned.1.call-done), kind=kOutput, calls=%fused_computation.34 | convolution fusion | flops 25769803776 | bytes 39845888 | tf_op jit(solution)/shard_map/dot_general | solution.py:14
  124.6 21.0 %all-gather.10.cloned.1.call-done = f32[4096,256]{1,0:T(8,128)} async-done(((f32[256,256]{1,0:T(8,128)}), f32[4096,256]{1,0:T(8,128)}) %all-gather.10.cloned.1.call-update) | async-done | bytes 4194320 | tf_op jit(solution)/shard_map/all_gather | solution.py:57
  145.7 33.0 %fusion.1 = f32[2048,256]{1,0:T(8,128)} fusion(f32[4096,256]{1,0:T(8,128)} %all-gather.10.cloned.1.call-done, f32[2048,4096]{1,0:T(8,128)} %fusion.13), kind=kOutput, calls=%fused_computation.2 | convolution fusion | flops 25794969600 | bytes 39845888 | tf_op jit(solution)/shard_map/dot_general | solution.py:59
  178.7 34.0 %reduce-scatter.4.cloned.1.call-done = f32[256,256]{1,0:T(8,128)} async-done(((f32[2048,256]{1,0:T(8,128)}), f32[256,256]{1,0:T(8,128)}) %reduce-scatter.4.cloned.1.call-update) | async-done | bytes 262160 | tf_op jit(solution)/shard_map/reduce_scatter | solution.py:58
  214.1 65.1 %all-reduce = (f32[4]{0:T(128)S(1)}, f32[4]{0:T(128)S(1)}) all-reduce(f32[4]{0:T(128)S(1)} %reduce_sum.67, f32[4]{0:T(128)S(1)} %reduce_sum.88), channel_id=1, replica_groups=mesh['row'=16,'col'=8] {'row','col'}, use_global_device_ids=true, to_apply=%region_2.3 | all-reduce | flops 8 | bytes 64 | tf_op jit(solution)/shard_map/psum | solution.py:49
  279.4 1.1 multiply_reduce_fusion.1
  280.7 62.0 %psum.30 = f32[4]{0:T(128)S(1)} all-reduce(f32[4]{0:T(128)S(1)} %reduce_sum.91), channel_id=1, replica_groups=mesh['row'=16,'col'=8] {'row','col'}, use_global_device_ids=true, to_apply=%region_10.11 | all-reduce | flops 4 | bytes 32 | tf_op jit(solution)/shard_map/psum | solution.py:49
  342.9 2.1 fusion.11
  345.1 48.6 %all-gather.12.cloned.1.call-done = f32[4096,256]{1,0:T(8,128)} async-done(((f32[256,256]{1,0:T(8,128)}), f32[4096,256]{1,0:T(8,128)}) %all-gather.12.cloned.1.call-update) | async-done | bytes 4194320 | tf_op jit(solution)/shard_map/all_gather | solution.py:57
  393.6 33.0 %fusion = f32[2048,256]{1,0:T(8,128)} fusion(f32[4096,256]{1,0:T(8,128)} %all-gather.12.cloned.1.call-done, f32[2048,4096]{1,0:T(8,128)} %fusion.13), kind=kOutput, calls=%fused_computation.1 | convolution fusion | flops 25794969600 | bytes 39845888 | tf_op jit(solution)/shard_map/dot_general | solution.py:59
  426.7 34.0 %reduce-scatter.6.cloned.1.call-done = f32[256,256]{1,0:T(8,128)} async-done(((f32[2048,256]{1,0:T(8,128)}), f32[256,256]{1,0:T(8,128)}) %reduce-scatter.6.cloned.1.call-update) | async-done | bytes 262160 | tf_op jit(solution)/shard_map/reduce_scatter | solution.py:58
  460.6 1.1 multiply_reduce_fusion
  461.9 65.0 %psum.31 = f32[4]{0:T(128)S(1)} all-reduce(f32[4]{0:T(128)S(1)} %reduce_sum.94), channel_id=1, replica_groups=mesh['row'=16,'col'=8] {'row','col'}, use_global_device_ids=true, to_apply=%region_14.15 | all-reduce | flops 4 | bytes 32 | tf_op jit(solution)/shard_map/psum | solution.py:65
  527.1 1.2 fusion.5
  528.6 13.3 %all_gather.22 = f32[512,256]{1,0:T(8,128)S(1)} all-gather(f32[64,256]{1,0:T(8,128)S(1)} %broadcast_divide_fusion.1), channel_id=1, replica_groups=mesh['row'=16,'col'=8] {'col'}, dimensions={0}, use_global_device_ids=true | all-gather | bytes 589824 | tf_op jit(solution)/shard_map/all_gather | solution.py:35
  541.9 10.8 %fusion.15 = f32[512,4096]{1,0:T(8,128)} fusion(f32[512,256]{1,0:T(8,128)S(1)} %all_gather.22, f32[4096,256]{1,0:T(8,128)} %all-gather.8.cloned.1.call-done), kind=kOutput, calls=%fused_computation.36 | convolution fusion | flops 6442450944 | bytes 13107200 | tf_op jit(solution)/shard_map/dot_general | solution.py:14
  552.7 23.1 %all-gather.14.cloned.1.call-done = f32[4096,256]{1,0:T(8,128)} async-done(((f32[256,256]{1,0:T(8,128)}), f32[4096,256]{1,0:T(8,128)}) %all-gather.14.cloned.1.call-update) | async-done | bytes 4194320 | tf_op jit(solution)/shard_map/all_gather | solution.py:74
  575.7 11.2 %fusion.2 = f32[512,256]{1,0:T(8,128)} fusion(f32[4096,256]{1,0:T(8,128)} %all-gather.14.cloned.1.call-done, f32[512,4096]{1,0:T(8,128)} %fusion.15), kind=kOutput, calls=%fused_computation.4 | convolution fusion | flops 6448742400 | bytes 13107200 | tf_op jit(solution)/shard_map/dot_general | solution.py:77
  587.8 30.5 %reduce-scatter.8.cloned.1.call-done = f32[64,256]{1,0:T(8,128)} async-done(((f32[512,256]{1,0:T(8,128)}), f32[64,256]{1,0:T(8,128)}) %reduce-scatter.8.cloned.1.call-update) | async-done | bytes 65552 | tf_op jit(solution)/shard_map/reduce_scatter | solution.py:76
  618.3 1.5 add.78
  (60 shorter events, 9.7 us)
Async XLA Ops:
  7.2 31.1 %all-gather.6.cloned.1.call-start = ((), (), s32[]{:S(2)}) async-start(), calls=%async_computation.3 | async-start | bytes 2359296 | tf_op jit(solution)/shard_map/all_gather | solution.py:34
  10.1 81.8 %all-gather.8.cloned.1.call-start = ((), (), s32[]{:S(2)}) async-start(), calls=%async_computation.4 | async-start | bytes 4456448 | tf_op jit(solution)/shard_map/all_gather | solution.py:37
  10.8 134.8 %all-gather.10.cloned.1.call-start = ((), (), s32[]{:S(2)}) async-start(), calls=%async_computation.5 | async-start | bytes 4456448 | tf_op jit(solution)/shard_map/all_gather | solution.py:57
  16.1 196.5 %reduce-scatter.4.cloned.1.call-start = ((), (), s32[]{:S(2)}) async-start(), calls=%async_computation.6 | async-start | bytes 2359296 | tf_op jit(solution)/shard_map/reduce_scatter | solution.py:58
  124.6 88.0 %copy-start.4 = (s32[256]{0:T(256)S(1)}, s32[256]{0:T(256)}, u32[]{:S(2)}) copy-start(s32[256]{0:T(256)} %param.11) | copy-start | bytes 3076
  178.6 215.0 %all-gather.12.cloned.1.call-start = ((), (), s32[]{:S(2)}) async-start(), calls=%async_computation.7 | async-start | bytes 4456448 | tf_op jit(solution)/shard_map/all_gather | solution.py:57
  345.0 115.6 %copy-start = (f32[256,256]{1,0:T(8,128)S(1)}, f32[256,256]{1,0:T(8,128)}, u32[]{:S(2)}) copy-start(f32[256,256]{1,0:T(8,128)} %reduce-scatter.4.cloned.1.call-done) | copy-start | bytes 786436
  345.0 115.6 %reduce-scatter.6.cloned.1.call-start = ((), (), s32[]{:S(2)}) async-start(), calls=%async_computation.8 | async-start | bytes 2359296 | tf_op jit(solution)/shard_map/reduce_scatter | solution.py:58
  426.6 101.7 %copy-start.2 = (f32[64,256]{1,0:T(8,128)S(1)}, f32[64,256]{1,0:T(8,128)}, u32[]{:S(2)}) copy-start(f32[64,256]{1,0:T(8,128)} %param.10) | copy-start | bytes 196612
  426.6 149.1 %all-gather.14.cloned.1.call-start = ((), (), s32[]{:S(2)}) async-start(), calls=%async_computation.9 | async-start | bytes 4456448 | tf_op jit(solution)/shard_map/all_gather | solution.py:74
  528.3 90.0 %reduce-scatter.8.cloned.1.call-start = ((), (), s32[]{:S(2)}) async-start(), calls=%async_computation.10 | async-start | bytes 589824 | tf_op jit(solution)/shard_map/reduce_scatter | solution.py:76
  552.7 34.3 %copy-start.1 = (f32[256,256]{1,0:T(8,128)S(1)}, f32[256,256]{1,0:T(8,128)}, u32[]{:S(2)}) copy-start(f32[256,256]{1,0:T(8,128)} %reduce-scatter.6.cloned.1.call-done) | copy-start | bytes 786436
  552.7 65.6 %copy-start.3 = (f32[64,256]{1,0:T(8,128)S(1)}, f32[64,256]{1,0:T(8,128)}, u32[]{:S(2)}) copy-start(f32[64,256]{1,0:T(8,128)} %param.15) | copy-start | bytes 196612
Sparse Core Ops, SparseCore 0:
  10.2 27.9 all-gather.5
  40.4 51.4 all-gather.7
  94.6 50.9 all-gather.9
  178.8 33.8 reduce-scatter.3
  345.1 48.4 all-gather.11
  426.7 33.8 reduce-scatter.5
  528.4 47.2 all-gather.13
  587.0 31.1 reduce-scatter.7
where the time goes:
time: 627 us
  waiting for transfers between devices  268 us (43%)
  blocking collectives  205 us (33%)
  matrix products  125 us (20%)
  between operations  14.2 us (2%)
  other arithmetic  11.2 us (2%)
    psum x2, blocking collectives, squares(): return lax.psum(per_sample(values, values), ('row', 'col'))  127 us
    all_gather x2, waiting for transfers between devices, shards(): spread = lax.all_gather(mixed, 'row', axis=0, tiled=True)  69.6 us
    reduce_scatter x2, waiting for transfers between devices, shards(): lax.psum_scatter(jnp.dot(kernel_tile, spread, precision=lax.Precision.HIG...  67.9 us
    dot_general x2, matrix products, shards(): jnp.dot(kernel_tile, spread, precision=lax.Precision.HIGHEST)  65.9 us
    psum x1, blocking collectives, shards(): curve = lax.psum(per_sample(direction, image), ('row', 'col'))  65 us
    all_gather x1, waiting for transfers between devices, shards(): column_set = lax.all_gather(normed, 'row', axis=0, tiled=True)  53.7 us
    dot_general x2, matrix products, kernel(): lax.dot_general(left, right, (((1,), (1,)), ((), ())), precision=lax.Prec...  43.5 us
    reduce_scatter x1, waiting for transfers between devices, shards(): lax.psum_scatter(jnp.dot(cross, gathered, precision=lax.Precision.HIGHEST...  30.5 us
  transfers between devices with their start and end apart: 8, of which 8 were waited for; matrix products, arithmetic and copies ran while one was open for 8% of the time, Pallas kernels for 0%

commit v1 on v0

v1 whole, which is shorter than its diff:
```python
import jax
import jax.numpy as jnp
from jax import lax
from jax.experimental import pallas as pl
from jax.experimental.pallas import tpu as pltpu
from jax.sharding import PartitionSpec as P


AXES = ("row", "col")
F32 = jnp.float32
BF16 = jnp.bfloat16


def index(x, y, z, core):
    return ((x % 4) * 4 + y % 4) * 8 + (z % 4) * 2 + core % 2


def shift(values, dx=0, dy=0, dz=0, core=0):
    pairs = [
        (index(x, y, z, k), index(x + dx, y + dy, z + dz, k + core))
        for x in range(4)
        for y in range(4)
        for z in range(4)
        for k in range(2)
    ]
    return lax.ppermute(values, AXES, pairs)


def ring(values, axis):
    half = values.shape[0] // 2
    below = shift(values, **{axis: 1})
    above = shift(values, **{axis: -1})
    first = shift(below[:half], **{axis: 1})
    second = shift(above[half:], **{axis: -1})
    return [values, below, above, first, second]


def join_kernel(*refs):
    start = 0
    for ref in refs[:-1]:
        refs[-1][start : start + ref.shape[0], :] = ref[...]
        start += ref.shape[0]


def join(parts):
    rows = sum(part.shape[0] for part in parts)
    return pl.pallas_call(
        join_kernel,
        out_shape=jax.ShapeDtypeStruct((rows, parts[0].shape[1]), F32),
        name="join",
    )(*parts)


def plane_half(values, near, far):
    return ring(join(ring(values, near)), far)


def plane_gather(values):
    middle = values.shape[0] // 2
    return [plane_half(values[:middle], "dx", "dy"), plane_half(values[middle:], "dy", "dx")]


OFFSETS = (0, -1, 1, 2)


def plane_order():
    row = lax.axis_index("row")
    x, y = row // 4, row % 4
    steps = [(near, far) for far in OFFSETS for near in OFFSETS]
    one = [(((x + 4 + near) % 4) * 4 + (y + 4 + far) % 4) * 2 for near, far in steps]
    two = [(((x + 4 + far) % 4) * 4 + (y + 4 + near) % 4) * 2 + 1 for near, far in steps]
    return jnp.stack(one + two).astype(jnp.int32)


def line_order(other):
    col = lax.axis_index("col")
    z, core = col // 2, (col + other) % 2
    return jnp.stack([((z + 4 + step) % 4) * 2 + core for step in OFFSETS]).astype(jnp.int32)


def split(values):
    high = values.astype(BF16)
    return high, (values - high.astype(F32)).astype(BF16)


def dot(first, second, dims=(((1,), (0,)), ((), ()))):
    return lax.dot_general(first, second, dims, preferred_element_type=F32)


def dot_split(first, second, dims=(((1,), (0,)), ((), ()))):
    return dot(first[0], second[0], dims) + (
        dot(first[0], second[1], dims) + dot(first[1], second[0], dims)
    )


def form_kernel(n, order, *refs):
    cols, rows, high_out, low_out, high_cols, low_cols, high_rows, low_rows = refs[:n], *refs[n:]
    step = pl.program_id(0)

    @pl.when(step == 0)
    def _():
        start = 0
        for ref in cols:
            high, low = split(ref[...])
            high_cols[start : start + ref.shape[0], :] = high
            low_cols[start : start + ref.shape[0], :] = low
            start += ref.shape[0]
        size = rows.shape[1]
        for i in range(4):
            high, low = split(rows[order[i]])
            high_rows[i * size : (i + 1) * size, :] = high
            low_rows[i * size : (i + 1) * size, :] = low

    width = high_out.shape[1]
    here = pl.ds(pl.multiple_of(step * width, width), width)
    inner = dot_split(
        (high_rows[...], low_rows[...]),
        (high_cols[here, :], low_cols[here, :]),
        (((1,), (1,)), ((), ())),
    )
    high, low = split(inner + inner * inner * inner)
    high_out[...] = high
    low_out[...] = low


def whole(part):
    return pl.BlockSpec(part.shape, lambda i, *_: (0,) * part.ndim)


def form(order, rows, cols, block):
    width = sum(part.shape[0] for part in cols)
    total, depth = 4 * rows.shape[1], rows.shape[2]
    tile = pl.BlockSpec((total, block), lambda i, *_: (0, i))
    return pl.pallas_call(
        lambda *refs: form_kernel(len(cols), *refs),
        grid_spec=pltpu.PrefetchScalarGridSpec(
            num_scalar_prefetch=1,
            grid=(width // block,),
            in_specs=[whole(part) for part in [*cols, rows]],
            out_specs=[tile, tile],
            scratch_shapes=[pltpu.VMEM((width, depth), BF16)] * 2
            + [pltpu.VMEM((total, depth), BF16)] * 2,
        ),
        out_shape=[jax.ShapeDtypeStruct((total, width), BF16)] * 2,
        cost_estimate=pl.CostEstimate(
            flops=6 * total * width * depth, bytes_accessed=4 * total * width, transcendentals=0
        ),
        name="form",
    )(order, *cols, rows)


def apply_kernel(n, order, values, *refs):
    tests, high_tile, low_tile, out, sums = refs[:n], *refs[n:]
    step = pl.program_id(0)
    count = high_tile.shape[1] // values.shape[1]
    part = jnp.concatenate([values[order[step * count + i]] for i in range(count)], axis=0)
    result = dot_split((high_tile[...], low_tile[...]), split(part))

    @pl.when(step == 0)
    def _():
        out[...] = result

    @pl.when(step > 0)
    def _():
        out[...] += result

    @pl.when(step == pl.num_programs(0) - 1)
    def _():
        sums[...] = jnp.zeros_like(sums)
        for j, test in enumerate(tests):
            size, block = test.shape[0] // 4, out.shape[0] // 4
            for i in range(4):
                product = test[i * size : (i + 1) * size, :] * out[i * block : i * block + size, :]
                sums[j : j + 1, :] += jnp.sum(product, axis=0, keepdims=True)


def apply(tile, block, order, values, *tests):
    total, width = tile[0].shape
    columns = values.shape[2]
    tiles = pl.BlockSpec((total, block), lambda i, *_: (0, i))
    out_shape = [
        jax.ShapeDtypeStruct((total, columns), F32),
        jax.ShapeDtypeStruct((8, columns), F32),
    ]
    return pl.pallas_call(
        lambda *refs: apply_kernel(len(tests), *refs),
        grid_spec=pltpu.PrefetchScalarGridSpec(
            num_scalar_prefetch=1,
            grid=(width // block,),
            in_specs=[whole(part) for part in [values, *tests]] + [tiles, tiles],
            out_specs=[whole(part) for part in out_shape],
        ),
        out_shape=out_shape,
        cost_estimate=pl.CostEstimate(
            flops=6 * total * width * columns, bytes_accessed=4 * total * width, transcendentals=0
        ),
        name="apply",
    )(order, values, *tests, *tile)


def total_sums(partial, samples):
    devices = lax.axis_size("row") * lax.axis_size("col")
    spread = jnp.broadcast_to(partial[None], (devices,) + partial.shape)
    sums = jnp.sum(lax.all_to_all(spread, AXES, 0, 0), axis=0)
    return jnp.sum(sums.reshape(partial.shape[0], samples, -1), axis=2)


def shards(
    features,
    new_features,
    lengths,
    targets,
    prior_train,
    noise_draw,
    prior_new,
    time_kernel,
    noise_var,
):
    checkpoints = time_kernel.shape[0]
    columns = prior_train.shape[1]
    samples = columns // checkpoints
    items = features.shape[0]
    block = items + new_features.shape[0]

    both = jnp.concatenate([features, new_features], axis=0)
    normed = both / jnp.sqrt(jnp.sum(both * both, axis=1, keepdims=True) + 1e-06)

    line = lax.axis_size("col")
    rows = lax.all_to_all(jnp.broadcast_to(normed[None], (line,) + normed.shape), "col", 0, 0)
    cols = [part for half in plane_gather(normed[:items]) for part in half]
    middle = block // 2

    mixing = jnp.kron(jnp.eye(samples, dtype=F32), time_kernel)

    def mix(values):
        return jnp.dot(values, mixing, precision=lax.Precision.HIGHEST)

    position = jnp.arange(columns, dtype=jnp.int32) % checkpoints
    mask = (position[None, :] < lengths[:, None]).astype(F32)
    noise_cols = jnp.tile(noise_var, samples)
    rhs = mask * (jnp.tile(targets, (1, samples)) - prior_train - jnp.sqrt(noise_cols) * noise_draw)
    plane = lax.axis_size("row")
    order = plane_order()

    def exchange(values):
        spread_out = jnp.broadcast_to(values[None], (plane, items, columns))
        received = lax.all_to_all(spread_out, "row", 0, 0)
        return received.reshape(2 * plane, items // 2, columns)

    def line_gather(values):
        own = join(ring(values, "dz"))
        return own, shift(own, core=1)

    def reduce_rows(own, other):
        received = shift(other, core=1)
        own, below, above, opposite = jnp.split(own + received, 4)
        up = shift(opposite[:middle], dz=1)
        down = shift(opposite[middle:], dz=-1)
        above = jnp.concatenate([above[:middle] + up, above[middle:]], axis=0)
        below = jnp.concatenate([below[:middle], below[middle:] + down], axis=0)
        own = own + (shift(above, dz=1) + shift(below, dz=-1))
        return own[:items], own[items:]

    def spread(scalars):
        return jnp.repeat(scalars, checkpoints)[None, :]

    def local_sums(*pairs):
        return [jnp.sum(first * second, axis=0) for first, second in pairs]

    mixed = exchange(mix(rhs))
    rhs_own, rhs_other = line_gather(rhs)
    tile_other = form(line_order(1), rows, cols, 256)
    tile_own = form(line_order(0), rows, cols, 256)
    other, sums_other = apply(tile_other, 1024, order, mixed, rhs_other)
    own, sums_own = apply(tile_own, 1024, order, mixed, rhs_own)
    norm_first, noise_first = local_sums((rhs, rhs), (rhs, noise_cols * rhs))
    curve_first = sums_own[0] + sums_other[0] + noise_first
    norm_first, curve_first = total_sums(jnp.stack([norm_first, curve_first]), samples)
    train, new_first = reduce_rows(own, other)
    image = mask * train + noise_cols * rhs
    step_first = norm_first / curve_first
    residual = rhs - spread(step_first) * image

    mixed = exchange(mix(residual))
    res_own, res_other = line_gather(residual)
    other, sums_other = apply(tile_other, 1024, order, mixed, rhs_other, res_other)
    own, sums_own = apply(tile_own, 1024, order, mixed, rhs_own, res_own)
    tests = sums_own + sums_other
    norm_next, res_image, noise_rhs, noise_res = local_sums(
        (residual, residual),
        (residual, image),
        (rhs, noise_cols * residual),
        (residual, noise_cols * residual),
    )
    partial = jnp.stack([norm_next, res_image, tests[0] + noise_rhs, tests[1] + noise_res])
    norm_next, res_image, rhs_answer, res_answer = total_sums(partial, samples)
    ratio = norm_next / norm_first
    curve_second = res_answer + ratio * (res_image + rhs_answer + ratio * curve_first)
    step_second = norm_next / curve_second
    train, new_second = reduce_rows(own, other)
    answer = mask * train + noise_cols * residual
    residual = residual - spread(step_second) * (answer + spread(ratio) * image)
    predicted = (
        prior_new
        + spread(step_first + step_second * ratio) * new_first
        + spread(step_second) * new_second
    )
    return (residual, predicted)


def solution(mesh):
    return jax.shard_map(
        shards,
        mesh=mesh,
        in_specs=(
            P(("row", "col"), None),
            P(("row", "col"), None),
            P(("row", "col")),
            P(("row", "col"), None),
            P(("row", "col"), None),
            P(("row", "col"), None),
            P(("row", "col"), None),
            P(),
            P(),
        ),
        out_specs=(P(("row", "col"), None), P(("row", "col"), None)),
        check_vma=False,
    )
```

time: 627 us -> 405 us (0.65)
  blocking collectives: 205 us -> 0 us
  matrix products: 125 us -> 1.47 us
  Pallas kernels: 0 us -> 112 us
  waiting for transfers between devices: 268 us -> 165 us
  starting transfers between devices: 0.33 us -> 92.6 us
  local copies, waits for them, and re-layouts: 2.9 us -> 18.7 us
  between operations: 14.2 us -> 1.45 us
    psum x3 -> x0, blocking collectives: 192 us -> none  [the longest x2 127 us: squares(): return lax.psum(per_sample(values, values), ('row', 'col'))]
    all_gather x5 -> x0, waiting for transfers between devices: 168 us -> none  [the longest x2 69.6 us: shards(): spread = lax.all_gather(mixed, 'row', axis=0, tiled=True)]
    dot_general x8 -> x2, matrix products: 125 us -> 1.47 us  [mix(): return jnp.dot(values, mixing, precision=lax.Precision.HIGHEST)]
    pallas_call x0 -> x10, Pallas kernels: none -> 112 us  [the longest x4 63.1 us: apply(): pl.pallas_call(lambda *refs: apply_kernel(len(tests), *refs), grid_spec=p...]
    reduce_scatter x3 -> x0, waiting for transfers between devices: 98.4 us -> none  [the longest x2 67.9 us: shards(): lax.psum_scatter(jnp.dot(kernel_tile, spread, precision=lax.Precision.HIG...]
    all_to_all x0 -> x5, waiting for transfers between devices: none -> 82.8 us  [the longest x2 40 us: exchange(): received = lax.all_to_all(spread_out, 'row', 0, 0)]
    ppermute x0 -> x36, waiting for transfers between devices: none -> 82.1 us  [shift(): return lax.ppermute(values, AXES, pairs)]
    ppermute x0 -> x36, starting transfers between devices: none -> 54.1 us  [shift(): return lax.ppermute(values, AXES, pairs)]
  transfers between devices with their start and end apart: 8 -> 41, of which waited for: 8 -> 16; matrix products, arithmetic and copies ran while one was open for 8% -> 4% of each run, Pallas kernels for 0% -> 20%
where the time goes in v1:
time: 405 us; the launch traced here: 404 us
  waiting for transfers between devices  165 us (41%)
  Pallas kernels  112 us (28%)
  starting transfers between devices  92.6 us (23%)
  local copies, waits for them, and re-layouts  18.7 us (5%)
  other arithmetic  12.8 us (3%)
    ppermute x36, waiting for transfers between devices, shift(): return lax.ppermute(values, AXES, pairs)  82.1 us
    pallas_call x4, Pallas kernels, apply(): pl.pallas_call(lambda *refs: apply_kernel(len(tests), *refs), grid_spec=p...  63.1 us
    ppermute x36, starting transfers between devices, shift(): return lax.ppermute(values, AXES, pairs)  54.1 us
    pallas_call x2, Pallas kernels, form(): pl.pallas_call(lambda *refs: form_kernel(len(cols), *refs), grid_spec=plt...  40.7 us
    all_to_all x2, waiting for transfers between devices, exchange(): received = lax.all_to_all(spread_out, 'row', 0, 0)  40 us
    all_to_all x1, waiting for transfers between devices, shards(): lax.all_to_all(jnp.broadcast_to(normed[None], (line,) + normed.shape), 'c...  27.1 us
    all_to_all x2, starting transfers between devices, total_sums(): sums = jnp.sum(lax.all_to_all(spread, AXES, 0, 0), axis=0)  19.4 us
    all_to_all x2, waiting for transfers between devices, total_sums(): sums = jnp.sum(lax.all_to_all(spread, AXES, 0, 0), axis=0)  15.7 us
  transfers between devices with their start and end apart: 41, of which 16 were waited for; matrix products, arithmetic and copies ran while one was open for 4% of the time, Pallas kernels for 20%

profile of v1, /device:TPU:0, one launch (start us, length us, event | category | flops | bytes accessed | tf_op | source)
XLA Modules:
  0.0 404.0 jit_solution(14733708465760664089)
XLA Ops:
  4.4 5.6 %all-to-all-start.1 = ((f32[8,320,256]{2,1,0:T(8,128)}), f32[8,320,256]{2,1,0:T(8,128)S(1)}, u32[]{:S(2)}, u32[]{:S(2)}) async-start(f32[8,320,256]{2,1,0:T(8,128)} %broadcast_in_dim.23), calls=%async_computation.1 | async-start | bytes 5242880 | tf_op jit(solution)/shard_map/all_to_all | solution.py:229
  15.7 27.1 %all-to-all-done.1.refs_11_ = f32[8,320,256]{2,1,0:T(8,128)S(1)} async-done(((f32[8,320,256]{2,1,0:T(8,128)}), f32[8,320,256]{2,1,0:T(8,128)S(1)}, u32[]{:S(2)}, u32[]{:S(2)}) %all-to-all-start.1) | async-done | bytes 2621472 | tf_op jit(solution)/shard_map/all_to_all | solution.py:229
  42.8 3.5 broadcast_in_dim.22
  46.3 7.1 %all-to-all-start = ((f32[16,256,256]{2,1,0:T(8,128)}), f32[16,256,256]{2,1,0:T(8,128)}, u32[]{:S(2)}, u32[]{:S(2)}) async-start(f32[16,256,256]{2,1,0:T(8,128)} %broadcast_in_dim.22), calls=%async_computation | async-start | bytes 8388608 | tf_op jit(solution)/shard_map/all_to_all | solution.py:247
  60.5 44.3 %collective-permute-done.5.refs_2_ = f32[128,256]{1,0:T(8,128)S(1)} collective-permute-done((f32[128,256]{1,0:T(8,128)S(1)}, f32[128,256]{1,0:T(8,128)S(1)}, u32[]{:S(2)}, u32[]{:S(2)}) %collective-permute-start.5) | collective-permute-done | bytes 131104 | tf_op jit(solution)/shard_map/ppermute | solution.py:26
  104.8 15.5 %collective-permute-start.7 = (f32[64,256]{1,0:T(8,128)S(1)}, f32[64,256]{1,0:T(8,128)S(1)}, u32[]{:S(2)}, u32[]{:S(2)}) collective-permute-start(f32[64,256]{1,0:T(8,128)S(1)} %slice.155), channel_id=1, source_target_pairs={{0,96},{1,97},{2,98},{3,99},{4,100},{5,101},{6,102},{7,103},{8,104... | collective-permute-start | bytes 196616 | tf_op jit(solution)/shard_map/ppermute | solution.py:26
  136.4 3.9 collective-permute-done.3.refs_4_
  142.4 4.2 %collective-permute-done.2.refs_3_ = f32[128,256]{1,0:T(8,128)S(1)} collective-permute-done((f32[128,256]{1,0:T(8,128)S(1)}, f32[128,256]{1,0:T(8,128)S(1)}, u32[]{:S(2)}, u32[]{:S(2)}) %collective-permute-start.2) | collective-permute-done | bytes 131104 | tf_op jit(solution)/shard_map/ppermute | solution.py:26
  152.2 3.3 collective-permute-start.19
  161.8 4.4 %collective-permute-done.18.refs_9_ = f32[256,256]{1,0:T(8,128)} collective-permute-done((f32[256,256]{1,0:T(8,128)S(1)}, f32[256,256]{1,0:T(8,128)}, u32[]{:S(2)}, u32[]{:S(2)}) %collective-permute-start.18) | collective-permute-done | bytes 262176 | tf_op jit(solution)/shard_map/ppermute | solution.py:26
  166.2 20.6 %form.3 = (bf16[1280,4096]{1,0:T(8,128)(2,1)}, bf16[1280,4096]{1,0:T(8,128)(2,1)}) custom-call(s32[4]{0:T(128)} %pad_add_fusion.1.refs_0_, f32[512,256]{1,0:T(8,128)} %join.5.refs_1_, f32[512,256]{1,0:T(8,128)} %copy-done.20, f32[512,256]{1,0:T(8,128)} %copy-done.19, f32[256,256]{1,0:T(8,128)} %copy-done.34, f32[256,256]{1,0:T(8,128)} %copy-done.33, ...), custom_call_target="tpu_custom_call" | custom-call | flops 8053063680 | bytes 20971520 | tf_op jit(solution)/shard_map/form/pallas_call | solution.py:134
  186.8 15.6 %apply.5 = (f32[1280,256]{1,0:T(8,128)}, f32[8,256]{1,0:T(8,128)}) custom-call(s32[32]{0:T(128)} %stack.180.refs_0_, f32[32,128,256]{2,1,0:T(8,128)} %bitcast.34.refs_1_, f32[1024,256]{1,0:T(8,128)} %collective-permute-done.20.refs_2_, bf16[1280,4096]{1,0:T(8,128)(2,1)} %get-tuple-element.17.refs_3_.refs_4_, bf16[1280,4096]{1,0:T(8,128)(2,1)} %get-tuple-element.18.refs_4_.refs_5_), custom_call_target="tpu_custom_call" | custom-call | flops 8053063680 | bytes 20971520 | tf_op jit(solution)/shard_map/apply/pallas_call | solution.py:185
  202.3 20.1 %form.2 = (bf16[1280,4096]{1,0:T(8,128)(2,1)}, bf16[1280,4096]{1,0:T(8,128)(2,1)}) custom-call(s32[4]{0:T(128)} %pad_add_fusion.refs_0_, f32[512,256]{1,0:T(8,128)} %join.5.refs_1_, f32[512,256]{1,0:T(8,128)} %copy-done.20, f32[512,256]{1,0:T(8,128)} %copy-done.19, f32[256,256]{1,0:T(8,128)} %copy-done.34, f32[256,256]{1,0:T(8,128)} %copy-done.33, ...), custom_call_target="tpu_custom_call" | custom-call | flops 8053063680 | bytes 20971520 | tf_op jit(solution)/shard_map/form/pallas_call | solution.py:134
  222.4 15.6 %apply.4 = (f32[1280,256]{1,0:T(8,128)}, f32[8,256]{1,0:T(8,128)}) custom-call(s32[32]{0:T(128)} %stack.180.refs_0_, f32[32,128,256]{2,1,0:T(8,128)} %bitcast.34.refs_1_, f32[1024,256]{1,0:T(8,128)} %join.4.refs_2_, bf16[1280,4096]{1,0:T(8,128)(2,1)} %get-tuple-element.14.refs_3_.refs_4_, bf16[1280,4096]{1,0:T(8,128)(2,1)} %get-tuple-element.15.refs_4_.refs_5_), custom_call_target="tpu_custom_call" | custom-call | flops 8053063680 | bytes 20971520 | tf_op jit(solution)/shard_map/apply/pallas_call | solution.py:185
  243.2 6.5 %all-to-all-start.2 = ((f32[128,2,256]{2,1,0:T(2,128)}), f32[128,2,256]{2,1,0:T(2,128)S(1)}, u32[]{:S(2)}, u32[]{:S(2)}) async-start(f32[128,2,256]{2,1,0:T(2,128)} %broadcast_in_dim.24), calls=%async_computation.2 | async-start | bytes 524288 | tf_op jit(solution)/shard_map/all_to_all | solution.py:204
  253.8 6.8 %all-to-all-done.2 = f32[128,2,256]{2,1,0:T(2,128)S(1)} async-done(((f32[128,2,256]{2,1,0:T(2,128)}), f32[128,2,256]{2,1,0:T(2,128)S(1)}, u32[]{:S(2)}, u32[]{:S(2)}) %all-to-all-start.2) | async-done | bytes 262176 | tf_op jit(solution)/shard_map/all_to_all | solution.py:204
  266.4 6.4 %all-to-all-start.3 = ((f32[16,256,256]{2,1,0:T(8,128)}), f32[16,256,256]{2,1,0:T(8,128)}, u32[]{:S(2)}, u32[]{:S(2)}) async-start(f32[16,256,256]{2,1,0:T(8,128)} %broadcast_in_dim.26), calls=%async_computation.3 | async-start | bytes 8388608 | tf_op jit(solution)/shard_map/all_to_all | solution.py:247
  275.0 6.0 %collective-permute-done.27.refs_2_ = f32[256,256]{1,0:T(8,128)S(1)} collective-permute-done((f32[256,256]{1,0:T(8,128)S(1)}, f32[256,256]{1,0:T(8,128)S(1)}, u32[]{:S(2)}, u32[]{:S(2)}) %collective-permute-start.27) | collective-permute-done | bytes 262176 | tf_op jit(solution)/shard_map/ppermute | solution.py:26
  286.0 3.5 collective-permute-done.28.refs_3_
  295.3 40.0 %all-to-all-done.3 = f32[16,256,256]{2,1,0:T(8,128)} async-done(((f32[16,256,256]{2,1,0:T(8,128)}), f32[16,256,256]{2,1,0:T(8,128)}, u32[]{:S(2)}, u32[]{:S(2)}) %all-to-all-start.3) | async-done | bytes 4194336 | tf_op jit(solution)/shard_map/all_to_all | solution.py:247
  335.3 15.9 %apply.7 = (f32[1280,256]{1,0:T(8,128)}, f32[8,256]{1,0:T(8,128)}) custom-call(s32[32]{0:T(128)} %stack.180.refs_0_, f32[32,128,256]{2,1,0:T(8,128)} %bitcast.48.refs_1_, f32[1024,256]{1,0:T(8,128)} %collective-permute-done.20.refs_2_, f32[1024,256]{1,0:T(8,128)} %copy-done.32, bf16[1280,4096]{1,0:T(8,128)(2,1)} %get-tuple-element.17.refs_3_.refs_4_, ...), custom_call_target="tpu_custom_call" | custom-call | flops 8053063680 | bytes 20971520 | tf_op jit(solution)/shard_map/apply/pallas_call | solution.py:185
  351.3 16.0 %apply.6 = (f32[1280,256]{1,0:T(8,128)}, f32[8,256]{1,0:T(8,128)}) custom-call(s32[32]{0:T(128)} %stack.180.refs_0_, f32[32,128,256]{2,1,0:T(8,128)} %bitcast.48.refs_1_, f32[1024,256]{1,0:T(8,128)} %join.4.refs_2_, f32[1024,256]{1,0:T(8,128)} %join.7.refs_3_, bf16[1280,4096]{1,0:T(8,128)(2,1)} %get-tuple-element.14.refs_3_.refs_4_, ...), custom_call_target="tpu_custom_call" | custom-call | flops 8053063680 | bytes 20971520 | tf_op jit(solution)/shard_map/apply/pallas_call | solution.py:185
  372.5 12.9 %all-to-all-start.4 = ((f32[128,4,256]{2,1,0:T(4,128)}), f32[128,4,256]{2,1,0:T(4,128)S(1)}, u32[]{:S(2)}, u32[]{:S(2)}) async-start(f32[128,4,256]{2,1,0:T(4,128)} %broadcast_in_dim.27), calls=%async_computation.4 | async-start | bytes 1048576 | tf_op jit(solution)/shard_map/all_to_all | solution.py:204
  390.2 8.9 %all-to-all-done.4 = f32[128,4,256]{2,1,0:T(4,128)S(1)} async-done(((f32[128,4,256]{2,1,0:T(4,128)}), f32[128,4,256]{2,1,0:T(4,128)S(1)}, u32[]{:S(2)}, u32[]{:S(2)}) %all-to-all-start.4) | async-done | bytes 524320 | tf_op jit(solution)/shard_map/all_to_all | solution.py:204
  (212 shorter events, 88.9 us)
Async XLA Ops:
  4.4 38.3 %all-to-all-start.1 = ((f32[8,320,256]{2,1,0:T(8,128)}), f32[8,320,256]{2,1,0:T(8,128)S(1)}, u32[]{:S(2)}, u32[]{:S(2)}) async-start(f32[8,320,256]{2,1,0:T(8,128)} %broadcast_in_dim.23), calls=%async_computation.1 | async-start | bytes 5242880 | tf_op jit(solution)/shard_map/all_to_all | solution.py:229
  46.3 140.5 %all-to-all-start = ((f32[16,256,256]{2,1,0:T(8,128)}), f32[16,256,256]{2,1,0:T(8,128)}, u32[]{:S(2)}, u32[]{:S(2)}) async-start(f32[16,256,256]{2,1,0:T(8,128)} %broadcast_in_dim.22), calls=%async_computation | async-start | bytes 8388608 | tf_op jit(solution)/shard_map/all_to_all | solution.py:247
  53.4 81.0 %collective-permute-start.1 = (f32[256,256]{1,0:T(8,128)S(1)}, f32[256,256]{1,0:T(8,128)S(1)}, u32[]{:S(2)}, u32[]{:S(2)}) collective-permute-start(f32[256,256]{1,0:T(8,128)S(1)} %get-tuple-element.36.refs_0_), channel_id=1, source_target_pairs={{0,6},{1,7},{2,0},{3,1},{4,2},{5,3},{6,4},{7,5},{8,14},{9,15},{10,... | collective-permute-start | bytes 786440 | tf_op jit(solution)/shard_map/ppermute | solution.py:26
  54.7 50.1 %collective-permute-start.5 = (f32[128,256]{1,0:T(8,128)S(1)}, f32[128,256]{1,0:T(8,128)S(1)}, u32[]{:S(2)}, u32[]{:S(2)}) collective-permute-start(f32[128,256]{1,0:T(8,128)S(1)} %get-tuple-element.50.refs_0_), channel_id=1, source_target_pairs={{0,96},{1,97},{2,98},{3,99},{4,100},{5,101},{6,102},{7,103},{8,104... | collective-permute-start | bytes 393224 | tf_op jit(solution)/shard_map/ppermute | solution.py:26
  57.8 62.5 %collective-permute-start.4 = (f32[128,256]{1,0:T(8,128)S(1)}, f32[128,256]{1,0:T(8,128)S(1)}, u32[]{:S(2)}, u32[]{:S(2)}) collective-permute-start(f32[128,256]{1,0:T(8,128)S(1)} %get-tuple-element.50.refs_0_), channel_id=1, source_target_pairs={{0,32},{1,33},{2,34},{3,35},{4,36},{5,37},{6,38},{7,39},{8,40},{9,... | collective-permute-start | bytes 393224 | tf_op jit(solution)/shard_map/ppermute | solution.py:26
  57.8 62.6 %collective-permute-start.13 = (f32[128,256]{1,0:T(8,128)S(1)}, f32[128,256]{1,0:T(8,128)S(1)}, u32[]{:S(2)}, u32[]{:S(2)}) collective-permute-start(f32[128,256]{1,0:T(8,128)S(1)} %get-tuple-element.49.refs_0_), channel_id=1, source_target_pairs={{0,24},{1,25},{2,26},{3,27},{4,28},{5,29},{6,30},{7,31},{8,0},{9,1... | collective-permute-start | bytes 393224 | tf_op jit(solution)/shard_map/ppermute | solution.py:26
  60.4 60.1 %collective-permute-start.12 = (f32[128,256]{1,0:T(8,128)S(1)}, f32[128,256]{1,0:T(8,128)S(1)}, u32[]{:S(2)}, u32[]{:S(2)}) collective-permute-start(f32[128,256]{1,0:T(8,128)S(1)} %get-tuple-element.49.refs_0_), channel_id=1, source_target_pairs={{0,8},{1,9},{2,10},{3,11},{4,12},{5,13},{6,14},{7,15},{8,16},{9,17... | collective-permute-start | bytes 393224 | tf_op jit(solution)/shard_map/ppermute | solution.py:26
  104.8 17.9 %collective-permute-start.7 = (f32[64,256]{1,0:T(8,128)S(1)}, f32[64,256]{1,0:T(8,128)S(1)}, u32[]{:S(2)}, u32[]{:S(2)}) collective-permute-start(f32[64,256]{1,0:T(8,128)S(1)} %slice.155), channel_id=1, source_target_pairs={{0,96},{1,97},{2,98},{3,99},{4,100},{5,101},{6,102},{7,103},{8,104... | collective-permute-start | bytes 196616 | tf_op jit(solution)/shard_map/ppermute | solution.py:26
  122.6 12.4 %collective-permute-start = (f32[256,256]{1,0:T(8,128)S(1)}, f32[256,256]{1,0:T(8,128)S(1)}, u32[]{:S(2)}, u32[]{:S(2)}) collective-permute-start(f32[256,256]{1,0:T(8,128)S(1)} %get-tuple-element.36.refs_0_), channel_id=1, source_target_pairs={{0,2},{1,3},{2,4},{3,5},{4,6},{5,7},{6,0},{7,1},{8,10},{9,11},{10,... | collective-permute-start | bytes 786440 | tf_op jit(solution)/shard_map/ppermute | solution.py:26
  128.4 21.1 %collective-permute-start.9 = (f32[512,256]{1,0:T(8,128)}, f32[512,256]{1,0:T(8,128)S(1)}, u32[]{:S(2)}, u32[]{:S(2)}) collective-permute-start(f32[512,256]{1,0:T(8,128)} %join.5.refs_1_), channel_id=1, source_target_pairs={{0,24},{1,25},{2,26},{3,27},{4,28},{5,29},{6,30},{7,31},{8,0},{9,1... | collective-permute-start | bytes 1572872 | tf_op jit(solution)/shard_map/ppermute | solution.py:26
  128.4 23.6 %collective-permute-start.8 = (f32[512,256]{1,0:T(8,128)}, f32[512,256]{1,0:T(8,128)S(1)}, u32[]{:S(2)}, u32[]{:S(2)}) collective-permute-start(f32[512,256]{1,0:T(8,128)} %join.5.refs_1_), channel_id=1, source_target_pairs={{0,8},{1,9},{2,10},{3,11},{4,12},{5,13},{6,14},{7,15},{8,16},{9,17... | collective-permute-start | bytes 1572872 | tf_op jit(solution)/shard_map/ppermute | solution.py:26
  133.0 19.1 %collective-permute-start.17 = (f32[512,256]{1,0:T(8,128)}, f32[512,256]{1,0:T(8,128)S(1)}, u32[]{:S(2)}, u32[]{:S(2)}) collective-permute-start(f32[512,256]{1,0:T(8,128)} %join.6.refs_6_), channel_id=1, source_target_pairs={{0,96},{1,97},{2,98},{3,99},{4,100},{5,101},{6,102},{7,103},{8,104... | collective-permute-start | bytes 1572872 | tf_op jit(solution)/shard_map/ppermute | solution.py:26
  134.4 21.1 %collective-permute-start.16 = (f32[512,256]{1,0:T(8,128)}, f32[512,256]{1,0:T(8,128)}, u32[]{:S(2)}, u32[]{:S(2)}) collective-permute-start(f32[512,256]{1,0:T(8,128)} %join.6.refs_6_), channel_id=1, source_target_pairs={{0,32},{1,33},{2,34},{3,35},{4,36},{5,37},{6,38},{7,39},{8,40},{9,... | collective-permute-start | bytes 1572872 | tf_op jit(solution)/shard_map/ppermute | solution.py:26
  149.5 37.3 %collective-permute-start.20 = (f32[1024,256]{1,0:T(8,128)}, f32[1024,256]{1,0:T(8,128)}, u32[]{:S(2)}, u32[]{:S(2)}) collective-permute-start(f32[1024,256]{1,0:T(8,128)} %join.4.refs_2_), channel_id=1, source_target_pairs={{0,1},{1,0},{2,3},{3,2},{4,5},{5,4},{6,7},{7,6},{8,9},{9,8},{10,11... | collective-permute-start | bytes 3145736 | tf_op jit(solution)/shard_map/ppermute | solution.py:26
  202.3 35.7 %collective-permute-start.21 = (f32[1280,256]{1,0:T(8,128)}, f32[1280,256]{1,0:T(8,128)S(1)}, u32[]{:S(2)}, u32[]{:S(2)}) collective-permute-start(f32[1280,256]{1,0:T(8,128)} %get-tuple-element.21), channel_id=1, source_target_pairs={{0,1},{1,0},{2,3},{3,2},{4,5},{5,4},{6,7},{7,6},{8,9},{9,8},{10,11... | collective-permute-start | bytes 3932168 | tf_op jit(solution)/shard_map/ppermute | solution.py:26
  243.2 17.4 %all-to-all-start.2 = ((f32[128,2,256]{2,1,0:T(2,128)}), f32[128,2,256]{2,1,0:T(2,128)S(1)}, u32[]{:S(2)}, u32[]{:S(2)}) async-start(f32[128,2,256]{2,1,0:T(2,128)} %broadcast_in_dim.24), calls=%async_computation.2 | async-start | bytes 524288 | tf_op jit(solution)/shard_map/all_to_all | solution.py:204
  249.8 13.6 %collective-permute-start.23 = (f32[320,256]{1,0:T(8,128)S(1)}, f32[320,256]{1,0:T(8,128)S(1)}, u32[]{:S(2)}, u32[]{:S(2)}) collective-permute-start(f32[320,256]{1,0:T(8,128)S(1)} %pad_maximum_fusion), channel_id=1, source_target_pairs={{0,2},{1,3},{2,4},{3,5},{4,6},{5,7},{6,0},{7,1},{8,10},{9,11},{10,... | collective-permute-start | bytes 983048 | tf_op jit(solution)/shard_map/ppermute | solution.py:26
  266.4 68.9 %all-to-all-start.3 = ((f32[16,256,256]{2,1,0:T(8,128)}), f32[16,256,256]{2,1,0:T(8,128)}, u32[]{:S(2)}, u32[]{:S(2)}) async-start(f32[16,256,256]{2,1,0:T(8,128)} %broadcast_in_dim.26), calls=%async_computation.3 | async-start | bytes 8388608 | tf_op jit(solution)/shard_map/all_to_all | solution.py:247
  351.2 16.7 %collective-permute-start.31 = (f32[1280,256]{1,0:T(8,128)}, f32[1280,256]{1,0:T(8,128)S(1)}, u32[]{:S(2)}, u32[]{:S(2)}) collective-permute-start(f32[1280,256]{1,0:T(8,128)} %get-tuple-element.25), channel_id=1, source_target_pairs={{0,1},{1,0},{2,3},{3,2},{4,5},{5,4},{6,7},{7,6},{8,9},{9,8},{10,11... | collective-permute-start | bytes 3932168 | tf_op jit(solution)/shard_map/ppermute | solution.py:26
  369.5 15.9 %collective-permute-start.34 = (f32[160,256]{1,0:T(8,128)S(1)}, f32[160,256]{1,0:T(8,128)S(1)}, u32[]{:S(2)}, u32[]{:S(2)}) collective-permute-start(f32[160,256]{1,0:T(8,128)S(1)} %get-tuple-element.38), channel_id=1, source_target_pairs={{0,6},{1,7},{2,0},{3,1},{4,2},{5,3},{6,4},{7,5},{8,14},{9,15},{10,... | collective-permute-start | bytes 491528 | tf_op jit(solution)/shard_map/ppermute | solution.py:26
  369.6 15.9 %collective-permute-start.32 = (f32[160,256]{1,0:T(8,128)S(1)}, f32[160,256]{1,0:T(8,128)S(1)}, u32[]{:S(2)}, u32[]{:S(2)}) collective-permute-start(f32[160,256]{1,0:T(8,128)S(1)} %get-tuple-element.40), channel_id=1, source_target_pairs={{0,2},{1,3},{2,4},{3,5},{4,6},{5,7},{6,0},{7,1},{8,10},{9,11},{10,... | collective-permute-start | bytes 491528 | tf_op jit(solution)/shard_map/ppermute | solution.py:26
  372.5 26.7 %all-to-all-start.4 = ((f32[128,4,256]{2,1,0:T(4,128)}), f32[128,4,256]{2,1,0:T(4,128)S(1)}, u32[]{:S(2)}, u32[]{:S(2)}) async-start(f32[128,4,256]{2,1,0:T(4,128)} %broadcast_in_dim.27), calls=%async_computation.4 | async-start | bytes 1048576 | tf_op jit(solution)/shard_map/all_to_all | solution.py:204
  386.3 16.1 %collective-permute-start.33 = (f32[320,256]{1,0:T(8,128)}, f32[320,256]{1,0:T(8,128)S(1)}, u32[]{:S(2)}, u32[]{:S(2)}) collective-permute-start(f32[320,256]{1,0:T(8,128)} %pad_maximum_fusion.2), channel_id=1, source_target_pairs={{0,2},{1,3},{2,4},{3,5},{4,6},{5,7},{6,0},{7,1},{8,10},{9,11},{10,... | collective-permute-start | bytes 983048 | tf_op jit(solution)/shard_map/ppermute | solution.py:26
  388.1 14.3 %collective-permute-start.35 = (f32[320,256]{1,0:T(8,128)}, f32[320,256]{1,0:T(8,128)S(1)}, u32[]{:S(2)}, u32[]{:S(2)}) collective-permute-start(f32[320,256]{1,0:T(8,128)} %pad_maximum_fusion.3), channel_id=1, source_target_pairs={{0,6},{1,7},{2,0},{3,1},{4,2},{5,3},{6,4},{7,5},{8,14},{9,15},{10,... | collective-permute-start | bytes 983048 | tf_op jit(solution)/shard_map/ppermute | solution.py:26
  (52 other events, 665.0 us)
